TPU v7x, 256 devices: a whole 4x4x8 slice. The times are simulated.
256 devices in a mesh: dp: 4 (over x), expert: 32 (over z, y), tensor: 2 (over core).
Axes of the slice: x: 4, y: 4, z: 8, core: 2. Of those that a mesh axis runs over, the one named last changes fastest.
Arguments:
- queries: bfloat16 [8192, 4096], P(('dp', 'expert'), 'tensor'), may hold values from -8 to 8
- fresh_keys: bfloat16 [8192, 512], P(('dp', 'expert'), 'tensor'), may hold values from -6 to 6
- fresh_values: bfloat16 [8192, 512], P(('dp', 'expert'), 'tensor'), may hold values from -6 to 6
- resident_keys: bfloat16 [128, 2048, 512], P(('dp', 'expert'), None, 'tensor'), may hold values from -8 to 8
- resident_values: bfloat16 [128, 2048, 512], P(('dp', 'expert'), None, 'tensor'), may hold values from -6 to 6
- out_weight: bfloat16 [4096, 2048], P('tensor', 'dp'), may hold values from -0.5 to 0.5
- residual: bfloat16 [8192, 2048], P(('dp', 'expert')), may hold values from -23 to 23
- norm_gain: float32 [2048], replicated, may hold values from 0.1 to 1.9
- expert_ids: int32 [8192, 8], P(('dp', 'expert')), may hold values from 0 to 127, all different within a row; in each aligned block of 64 rows (0 to 63, 64 to 127, ...) at most 6 rows name the same one
- gates: float32 [8192, 8], P(('dp', 'expert')), may hold values from 0.05 to 0.5
- w_gate: bfloat16 [128, 2048, 768], P(('dp', 'expert'), None, 'tensor'), may hold values from -0.125 to 0.125
- w_up: bfloat16 [128, 2048, 768], P(('dp', 'expert'), None, 'tensor'), may hold values from -0.125 to 0.125
- w_down: bfloat16 [128, 768, 2048], P(('dp', 'expert'), 'tensor'), may hold values from -0.21875 to 0.21875
Outputs:
- mixed: bfloat16 [8192, 2048], P(('dp', 'expert'), 'tensor')
Inputs may be any that keep to these rules, and one draw needn't show every extreme that they name: `expert_ids`: within the 64 tokens of one sequence no expert is named by more than 6 tokens, a bound that some block reaches; a token names 8 different experts.
All inputs are finite; a program needn't handle non-finite values.
Results may differ from a plain program's by a relative error of at most 0.0085.
Values may be sent and summed in bfloat16 or wider, within the bound.
No kernel may reach another device: no remote copies, remote signals or barrier semaphores. Data moves between devices by JAX's collectives and lax.ppermute only.
A program may use at most 64 MiB of HBM per device.

v0:
```python
import jax
import jax.numpy as jnp
from jax import lax
from jax.sharding import PartitionSpec as P

D = 2048
HEAD_WIDTH = 128
CAP = 6


def attend_local(queries, fresh_keys, fresh_values, resident_keys, resident_values):
    tokens_here = queries.shape[0]
    kv_here = fresh_keys.shape[1] // HEAD_WIDTH
    query_group = queries.shape[1] // HEAD_WIDTH // kv_here
    context = resident_keys.shape[1]
    query_rows = queries.reshape(tokens_here, kv_here, query_group, HEAD_WIDTH)
    joined_keys = jnp.concatenate([resident_keys[0], fresh_keys], 0).reshape(
        context + tokens_here, kv_here, HEAD_WIDTH
    )
    joined_values = jnp.concatenate([resident_values[0], fresh_values], 0).reshape(
        context + tokens_here, kv_here, HEAD_WIDTH
    )
    score = jnp.einsum(
        "tjgd,sjd->jgts", query_rows, joined_keys, preferred_element_type=jnp.float32
    ) * HEAD_WIDTH ** (-0.5)
    places = jnp.arange(context + tokens_here)
    rows = jnp.arange(tokens_here)
    allowed = (places[None, :] < context) | (places[None, :] - context <= rows[:, None])
    score = jnp.where(allowed, score, jnp.float32(-1e30))
    top_score = jnp.max(score, axis=-1, keepdims=True)
    weight = jnp.exp(score - top_score)
    probs = (weight / jnp.sum(weight, axis=-1, keepdims=True)).astype(jnp.bfloat16)
    attended = jnp.einsum(
        "jgts,sjd->tjgd", probs, joined_values, preferred_element_type=jnp.float32
    )
    return attended.reshape(tokens_here, -1).astype(jnp.bfloat16)


def swap_pair(x):
    return lax.ppermute(x, "tensor", [(0, 1), (1, 0)])


def per_device(
    queries,
    fresh_keys,
    fresh_values,
    resident_keys,
    resident_values,
    out_weight,
    residual,
    norm_gain,
    expert_ids,
    gates,
    w_gate,
    w_up,
    w_down,
):
    tokens_here = residual.shape[0]
    lane = lax.axis_index("tensor")
    half = D // lax.axis_size("tensor")
    groups = lax.axis_size("dp")
    attended = attend_local(queries, fresh_keys, fresh_values, resident_keys, resident_values)
    gathered = lax.all_gather(attended, "dp", axis=0, tiled=True)
    part = jnp.dot(gathered, out_weight, preferred_element_type=jnp.float32)
    part = part.reshape(groups, tokens_here, -1)
    mine = lax.all_to_all(part, "dp", split_axis=0, concat_axis=0, tiled=True)
    mine = mine.transpose(1, 0, 2).reshape(tokens_here, D)
    summed = mine + swap_pair(mine)
    hidden = residual.astype(jnp.float32) + summed
    mean_square = jnp.mean(hidden * hidden, axis=-1, keepdims=True)
    normed = (hidden * lax.rsqrt(mean_square + 1e-06) * norm_gain).astype(jnp.bfloat16)
    hidden_half = lax.dynamic_slice_in_dim(hidden, lane * half, half, 1)
    normed_half = lax.dynamic_slice_in_dim(normed, lane * half, half, 1)
    owners = lax.axis_size("dp") * lax.axis_size("expert")
    onehot = (expert_ids[:, :, None] == jnp.arange(owners)[None, None, :]).astype(jnp.int32)
    per_token = jnp.sum(onehot, axis=1)
    before = jnp.cumsum(per_token, axis=0) - per_token
    slot = jnp.sum(onehot * before[:, None, :], axis=-1)
    code = expert_ids * CAP + slot
    pick = (code[:, :, None] == jnp.arange(owners * CAP)[None, None, :]).astype(jnp.bfloat16)
    spread = jnp.sum(pick, axis=1)
    outgoing = jnp.einsum(
        "tr,tf->rf", spread, normed_half, preferred_element_type=jnp.float32
    ).astype(jnp.bfloat16)
    received = lax.all_to_all(
        outgoing.reshape(owners, CAP, half),
        ("dp", "expert"),
        split_axis=0,
        concat_axis=0,
        tiled=True,
    ).reshape(owners * CAP, half)
    other = swap_pair(received)
    first = jnp.where(lane == 0, received, other)
    second = jnp.where(lane == 0, other, received)
    flat = jnp.concatenate([first, second], axis=1)
    gate_part = jnp.dot(flat, w_gate[0], preferred_element_type=jnp.float32)
    up_part = jnp.dot(flat, w_up[0], preferred_element_type=jnp.float32)
    act = (jax.nn.silu(gate_part) * up_part).astype(jnp.bfloat16)
    result = jnp.dot(act, w_down[0], preferred_element_type=jnp.float32)
    own = lax.dynamic_slice_in_dim(result, lane * half, half, 1)
    theirs = lax.dynamic_slice_in_dim(result, (1 - lane) * half, half, 1)
    expert_out = (own + swap_pair(theirs)).astype(jnp.bfloat16)
    returned = lax.all_to_all(
        expert_out.reshape(owners, CAP, half),
        ("dp", "expert"),
        split_axis=0,
        concat_axis=0,
        tiled=True,
    ).reshape(owners * CAP, half)
    picked = jnp.einsum("tkr,rf->tkf", pick, returned, preferred_element_type=jnp.float32)
    moe = jnp.sum(gates[:, :, None] * picked, axis=1)
    return (hidden_half + moe).astype(jnp.bfloat16)


def solution(mesh):
    return jax.shard_map(
        per_device,
        mesh=mesh,
        in_specs=(
            P(("dp", "expert"), "tensor"),
            P(("dp", "expert"), "tensor"),
            P(("dp", "expert"), "tensor"),
            P(("dp", "expert"), None, "tensor"),
            P(("dp", "expert"), None, "tensor"),
            P("tensor", "dp"),
            P(("dp", "expert"), None),
            P(),
            P(("dp", "expert"), None),
            P(("dp", "expert"), None),
            P(("dp", "expert"), None, "tensor"),
            P(("dp", "expert"), None, "tensor"),
            P(("dp", "expert"), "tensor", None),
        ),
        out_specs=P(("dp", "expert"), "tensor"),
        check_vma=False,
    )
```

profile of v0, /device:TPU:2, one launch (start us, length us, event | category | flops | bytes accessed | tf_op | source)
XLA Modules:
  0.0 256.4 jit_solution(13007185668899665555)
XLA Ops:
  6.5 0.0 copy-start
  6.5 0.0 all-gather.2.cloned.1.call-start
  6.5 0.6 iota_add_fusion
  7.1 1.5 copy.47
  8.7 1.3 copy.48
  10.0 0.0 copy-done.5
  10.0 0.8 copy.62
  10.8 1.5 copy.44
  12.3 1.3 copy.45
  13.7 0.0 copy-done.8
  13.7 0.0 copy-done.9
  13.7 0.6 copy_bitcast_fusion.1
  14.3 0.8 fusion.27
  15.1 0.0 copy-done.6
  15.1 0.0 copy-start.4
  15.1 4.7 %fusion.48 = f32[2,8,64]{2,1,0:T(8,128)S(1)} fusion(pred[64,2112]{1,0:T(8,128)(4,1)S(1)} %fusion.27, bf16[64,2,128]{2,0,1:T(8,128)(2,1)} %get-tuple-element.9, bf16[2048,2,128]{2,0,1:T(8,128)(2,1)} %copy.48, bf16[64,2,8,128]{3,2,1,0:T(8,128)(2,1)S(1)} %bitcast.82), kind=kOutput, calls=%fused_computation.65 | convolution fusion | flops 564463680 | bytes 1482752 | tf_op jit(solution)/shard_map/sub | solution.py:31
  19.8 0.0 copy-done.4
  19.8 5.6 %fusion.14 = bf16[64,2,8,128]{3,0,2,1:T(8,128)(2,1)} fusion(f32[2,8,64]{2,1,0:T(8,128)S(1)} %fusion.48, bf16[64,2,128]{2,0,1:T(8,128)(2,1)} %get-tuple-element.10, bf16[2048,2,128]{2,0,1:T(8,128)(2,1)} %copy.45, pred[64,2112]{1,0:T(8,128)(4,1)S(1)} %fusion.27, bf16[64,2,128]{2,0,1:T(8,128)(2,1)} %get-tuple-element.9, ...), kind=kOutput, calls=%fused_computation.25 | convolution fusion | flops 1122569216 | bytes 2826240 | tf_op jit(solution)/shard_map/jgts,sjd->tjgd/dot_general | solution.py:33
  25.4 1.1 copy.51
  26.5 0.8 copy.78
  27.3 0.0 all-gather.2.cloned.1.call-update
  27.3 0.0 copy-start.10
  27.4 28.6 %all-gather.2.cloned.1.call-done = bf16[256,2048]{1,0:T(8,128)(2,1)} async-done(((bf16[64,2048]{1,0:T(8,128)(2,1)}), bf16[256,2048]{1,0:T(8,128)(2,1)}) %all-gather.2.cloned.1.call-update) | async-done | bytes 1048592 | tf_op jit(solution)/shard_map/all_gather | solution.py:63
  55.9 0.0 copy-done
  55.9 2.7 %fusion.51 = f32[256,512]{1,0:T(8,128)} fusion(bf16[256,2048]{1,0:T(8,128)(2,1)} %all-gather.2.cloned.1.call-done, bf16[2048,512]{1,0:T(8,128)(2,1)S(1)} %copy-done), kind=kOutput, calls=%fused_computation.66 | convolution fusion | flops 536870912 | bytes 3670016 | tf_op jit(solution)/shard_map/dot_general | solution.py:64
  58.7 5.3 %all-to-all-start = ((f32[4,64,512]{2,1,0:T(8,128)}), f32[4,64,512]{2,1,0:T(8,128)S(1)}, u32[]{:S(2)}, u32[]{:S(2)}) async-start(f32[4,64,512]{2,1,0:T(8,128)} %bitcast.8), calls=%async_computation | async-start | bytes 1048576 | tf_op jit(solution)/shard_map/all_to_all | solution.py:66
  63.9 0.0 copy-done.10
  64.0 0.1 copy.54
  64.0 6.5 %all-to-all-done = f32[4,64,512]{2,1,0:T(8,128)S(1)} async-done(((f32[4,64,512]{2,1,0:T(8,128)}), f32[4,64,512]{2,1,0:T(8,128)S(1)}, u32[]{:S(2)}, u32[]{:S(2)}) %all-to-all-start) | async-done | bytes 524320 | tf_op jit(solution)/shard_map/all_to_all | solution.py:66
  70.6 0.3 collective-permute-start
  70.9 0.1 convert_reduce_fusion
  71.1 0.1 reduce_window_sum.11
  71.2 1.2 select_reduce_fusion
  72.4 0.1 copy.55
  72.5 0.1 copy.56
  72.6 0.0 copy-done.12
  72.6 0.5 fusion.19
  73.1 0.0 collective-permute-done
  73.1 0.0 copy-done.7
  73.2 1.2 multiply_reduce_fusion.1
  74.4 1.8 convolution_convert_fusion
  76.2 3.7 %reshape.67 = bf16[128,6,1024]{2,1,0:T(8,128)(2,1)} reshape(bf16[768,1024]{1,0:T(8,128)(2,1)} %convolution_convert_fusion) | data formatting | bytes 3145728 | tf_op jit(solution)/shard_map/reshape | solution.py:86
  79.9 64.9 %all_to_all.15 = bf16[128,6,1024]{2,1,0:T(8,128)(2,1)} all-to-all(bf16[128,6,1024]{2,1,0:T(8,128)(2,1)} %reshape.67), channel_id=1, replica_groups=mesh['dp'=4,'expert'=32,'tensor'=2] {'dp','expert'}, dimensions={0} | all-to-all | bytes 3145728 | tf_op jit(solution)/shard_map/all_to_all | solution.py:85
  144.8 3.7 %reshape.68 = bf16[768,1024]{1,0:T(8,128)(2,1)} reshape(bf16[128,6,1024]{2,1,0:T(8,128)(2,1)} %all_to_all.15) | data formatting | bytes 3145728 | tf_op jit(solution)/shard_map/reshape | solution.py:91
  148.5 0.0 collective-permute-start.1
  148.5 3.7 %collective-permute-done.1 = bf16[768,1024]{1,0:T(8,128)(2,1)} collective-permute-done((bf16[768,1024]{1,0:T(8,128)(2,1)}, bf16[768,1024]{1,0:T(8,128)(2,1)}, u32[]{:S(2)}, u32[]{:S(2)}) %collective-permute-start.1) | collective-permute-done | bytes 1572896 | tf_op jit(solution)/shard_map/ppermute | solution.py:40
  152.3 2.1 broadcast_select_fusion.1
  154.4 1.2 copy-done.2
  155.6 0.4 copy-done.3
  156.0 2.8 %fusion.6 = f32[768,384]{1,0:T(8,128)} fusion(bf16[768,1024]{1,0:T(8,128)(2,1)S(1)} %get-tuple-element.8, bf16[768,1024]{1,0:T(8,128)(2,1)S(1)} %get-tuple-element.7, bf16[1,2048,384]{2,1,0:T(8,128)(2,1)S(1)} %copy-done.13), kind=kOutput, calls=%fused_computation.12 | convolution fusion | flops 1214251008 | bytes 5898240 | tf_op jit(solution)/shard_map/dot_general | solution.py:97
  158.8 9.3 %fusion.8 = f32[768,2048]{1,0:T(8,128)} fusion(bf16[1,384,2048]{2,1,0:T(8,128)(2,1)} %param.25, f32[768,384]{1,0:T(8,128)} %fusion.6, bf16[768,1024]{1,0:T(8,128)(2,1)} %copy-done.3, bf16[768,1024]{1,0:T(8,128)(2,1)} %copy-done.2, bf16[1,2048,384]{2,1,0:T(8,128)(2,1)} %param.23), kind=kOutput, calls=%fused_computation.15 | convolution fusion | flops 2423980032 | bytes 13762560 | tf_op jit(solution)/shard_map/dot_general | solution.py:99
  168.0 2.3 constant_dynamic-slice_fusion
  170.3 0.2 collective-permute-start.2
  170.5 5.5 %collective-permute-done.2 = f32[768,1024]{1,0:T(8,128)S(1)} collective-permute-done((f32[768,1024]{1,0:T(8,128)S(1)}, f32[768,1024]{1,0:T(8,128)S(1)}, u32[]{:S(2)}, u32[]{:S(2)}) %collective-permute-start.2) | collective-permute-done | bytes 3145760 | tf_op jit(solution)/shard_map/ppermute | solution.py:40
  176.1 0.0 copy-done.1
  176.1 1.7 add_convert_fusion
  177.7 3.7 %reshape.69 = bf16[128,6,1024]{2,1,0:T(8,128)(2,1)} reshape(bf16[768,1024]{1,0:T(8,128)(2,1)} %add_convert_fusion) | data formatting | bytes 3145728 | tf_op jit(solution)/shard_map/reshape | solution.py:104
  181.4 9.0 %all-to-all-start.2 = ((bf16[128,6,1024]{2,1,0:T(8,128)(2,1)}), bf16[128,6,1024]{2,1,0:T(8,128)(2,1)}, u32[]{:S(2)}, u32[]{:S(2)}) async-start(bf16[128,6,1024]{2,1,0:T(8,128)(2,1)} %reshape.69), calls=%async_computation.2 | async-start | bytes 4194304 | tf_op jit(solution)/shard_map/all_to_all | solution.py:103
  190.5 0.0 copy-done.11
  190.5 0.1 copy.53
  190.6 51.7 %all-to-all-done.2 = bf16[128,6,1024]{2,1,0:T(8,128)(2,1)} async-done(((bf16[128,6,1024]{2,1,0:T(8,128)(2,1)}), bf16[128,6,1024]{2,1,0:T(8,128)(2,1)}, u32[]{:S(2)}, u32[]{:S(2)}) %all-to-all-start.2) | async-done | bytes 1572896 | tf_op jit(solution)/shard_map/all_to_all | solution.py:103
  242.3 3.7 %reshape.73 = bf16[768,1024,1]{1,0,2:T(8,128)(2,1)} reshape(bf16[128,6,1024]{2,1,0:T(8,128)(2,1)} %all-to-all-done.2) | data formatting | bytes 3145728 | tf_op jit(solution)/shard_map/reshape | solution.py:109
  246.0 2.8 %multiply_reduce_fusion = f32[64,1024]{1,0:T(8,128)S(1)} fusion(bf16[768,1024,1]{1,0,2:T(8,128)(2,1)} %reshape.73, f32[64,8]{1,0:T(8,128)S(1)} %copy.53, s32[64,8]{1,0:T(8,128)S(1)} %copy.56), kind=kOutput, calls=%fused_computation.11 | convolution fusion | flops 806682624 | bytes 1839104 | tf_op jit(solution)/shard_map/tkr,rf->tkf/dot_general | solution.py:110
  248.8 0.7 add_convert_fusion.1
  (18 shorter events, 0.1 us)
Async XLA Ops:
  6.5 49.4 %copy-start = (bf16[2048,512]{1,0:T(8,128)(2,1)S(1)}, bf16[2048,512]{1,0:T(8,128)(2,1)}, u32[]{:S(2)}) copy-start(bf16[2048,512]{1,0:T(8,128)(2,1)} %param.18) | copy-start | bytes 6291460
  6.5 49.4 %all-gather.2.cloned.1.call-start = ((), (), s32[]{:S(2)}) async-start(), calls=%async_computation.3 | async-start | bytes 1310720 | tf_op jit(solution)/shard_map/all_gather | solution.py:63
  7.1 2.9 %copy-start.5 = (bf16[64,2048]{1,0:T(8,128)(2,1)S(1)}, bf16[64,2048]{1,0:T(8,128)(2,1)}, u32[]{:S(2)}) copy-start(bf16[64,2048]{1,0:T(8,128)(2,1)} %param.13) | copy-start | bytes 786436
  10.8 2.9 %copy-start.8 = (bf16[64,256]{1,0:T(8,128)(2,1)S(1)}, bf16[64,256]{1,0:T(8,128)(2,1)}, u32[]{:S(2)}) copy-start(bf16[64,256]{1,0:T(8,128)(2,1)} %param.15) | copy-start | bytes 98308
  10.8 2.9 %copy-start.9 = (bf16[64,256]{1,0:T(8,128)(2,1)S(1)}, bf16[64,256]{1,0:T(8,128)(2,1)}, u32[]{:S(2)}) copy-start(bf16[64,256]{1,0:T(8,128)(2,1)} %param.14) | copy-start | bytes 98308
  10.8 4.3 %copy-start.6 = (bf16[8,8,16,128]{3,2,1,0:T(8,128)(2,1)S(1)}, bf16[8,8,16,128]{3,2,1,0:T(8,128)(2,1)}, u32[]{:S(2)}) copy-start(bf16[8,8,16,128]{3,2,1,0:T(8,128)(2,1)} %copy.62) | copy-start | bytes 786436
  15.1 4.7 %copy-start.4 = (bf16[2048,2,128]{2,0,1:T(8,128)(2,1)S(1)}, bf16[2048,2,128]{2,0,1:T(8,128)(2,1)}, u32[]{:S(2)}) copy-start(bf16[2048,2,128]{2,0,1:T(8,128)(2,1)} %copy.48) | copy-start | bytes 3145732
  27.3 36.6 %copy-start.10 = (s32[64,8]{0,1:T(8,128)S(1)}, s32[64,8]{0,1:T(8,128)}, u32[]{:S(2)}) copy-start(s32[64,8]{0,1:T(8,128)} %param.21) | copy-start | bytes 6148
  58.7 13.9 %copy-start.12 = (f32[2048]{0:T(1024)S(1)}, f32[2048]{0:T(1024)}, u32[]{:S(2)}) copy-start(f32[2048]{0:T(1024)} %param.20) | copy-start | bytes 24580
  58.7 14.5 %copy-start.7 = (bf16[64,2048]{1,0:T(8,128)(2,1)S(1)}, bf16[64,2048]{1,0:T(8,128)(2,1)}, u32[]{:S(2)}) copy-start(bf16[64,2048]{1,0:T(8,128)(2,1)} %param.19) | copy-start | bytes 786436
  58.7 11.9 %all-to-all-start = ((f32[4,64,512]{2,1,0:T(8,128)}), f32[4,64,512]{2,1,0:T(8,128)S(1)}, u32[]{:S(2)}, u32[]{:S(2)}) async-start(f32[4,64,512]{2,1,0:T(8,128)} %bitcast.8), calls=%async_computation | async-start | bytes 1048576 | tf_op jit(solution)/shard_map/all_to_all | solution.py:66
  70.6 2.5 collective-permute-start
  148.5 3.8 %collective-permute-start.1 = (bf16[768,1024]{1,0:T(8,128)(2,1)}, bf16[768,1024]{1,0:T(8,128)(2,1)}, u32[]{:S(2)}, u32[]{:S(2)}) collective-permute-start(bf16[768,1024]{1,0:T(8,128)(2,1)} %reshape.68), channel_id=1, source_target_pairs={{0,1},{1,0},{2,3},{3,2},{4,5},{5,4},{6,7},{7,6},{8,9},{9,8},{10,11... | collective-permute-start | bytes 4718600 | tf_op jit(solution)/shard_map/ppermute | solution.py:40
  148.5 7.5 %copy-start.13 = (bf16[1,2048,384]{2,1,0:T(8,128)(2,1)S(1)}, bf16[1,2048,384]{2,1,0:T(8,128)(2,1)}, u32[]{:S(2)}) copy-start(bf16[1,2048,384]{2,1,0:T(8,128)(2,1)} %param.24) | copy-start | bytes 4718596
  154.3 1.2 copy-start.2
  154.4 1.6 copy-start.3
  168.0 8.0 %copy-start.1 = (f32[768,2048]{1,0:T(8,128)S(1)}, f32[768,2048]{1,0:T(8,128)}, u32[]{:S(2)}) copy-start(f32[768,2048]{1,0:T(8,128)} %fusion.8) | copy-start | bytes 18874372
  170.3 5.7 %collective-permute-start.2 = (f32[768,1024]{1,0:T(8,128)S(1)}, f32[768,1024]{1,0:T(8,128)S(1)}, u32[]{:S(2)}, u32[]{:S(2)}) collective-permute-start(f32[768,1024]{1,0:T(8,128)S(1)} %constant_dynamic-slice_fusion), channel_id=1, source_target_pairs={{0,1},{1,0},{2,3},{3,2},{4,5},{5,4},{6,7},{7,6},{8,9},{9,8},{10,11... | collective-permute-start | bytes 9437192 | tf_op jit(solution)/shard_map/ppermute | solution.py:40
  181.4 9.0 %copy-start.11 = (f32[64,8]{0,1:T(8,128)S(1)}, f32[64,8]{0,1:T(8,128)}, u32[]{:S(2)}) copy-start(f32[64,8]{0,1:T(8,128)} %param.22) | copy-start | bytes 6148
  181.4 60.9 %all-to-all-start.2 = ((bf16[128,6,1024]{2,1,0:T(8,128)(2,1)}), bf16[128,6,1024]{2,1,0:T(8,128)(2,1)}, u32[]{:S(2)}, u32[]{:S(2)}) async-start(bf16[128,6,1024]{2,1,0:T(8,128)(2,1)} %reshape.69), calls=%async_computation.2 | async-start | bytes 4194304 | tf_op jit(solution)/shard_map/all_to_all | solution.py:103
Sparse Core Ops, SparseCore 0:
  27.5 28.4 all-gather.1
where the time goes:
time: 257 us; the launch traced here: 256 us
  waiting for transfers between devices  96.2 us (37%)
  blocking collectives  64.9 us (25%)
  matrix products  29.7 us (12%)
  local copies, waits for them, and re-layouts  28.1 us (11%)
  starting transfers between devices  14.8 us (6%)
  between operations  13.6 us (5%)
  other arithmetic  9.14 us (4%)
    all_to_all x1, blocking collectives, per_device(): lax.all_to_all(outgoing.reshape(owners, CAP, half), ('dp', 'expert'), spl...  64.9 us
    all_to_all x1, waiting for transfers between devices, per_device(): lax.all_to_all(expert_out.reshape(owners, CAP, half), ('dp', 'expert'), s...  51.7 us
    all_gather x1, waiting for transfers between devices, per_device(): gathered = lax.all_gather(attended, 'dp', axis=0, tiled=True)  28.6 us
    dot_general x1, matrix products, per_device(): result = jnp.dot(act, w_down[0], preferred_element_type=jnp.float32)  9.28 us
    ppermute x3, waiting for transfers between devices, swap_pair(): return lax.ppermute(x, 'tensor', [(0, 1), (1, 0)])  9.27 us
    all_to_all x1, starting transfers between devices, per_device(): lax.all_to_all(expert_out.reshape(owners, CAP, half), ('dp', 'expert'), s...  9.03 us
    all_to_all x1, waiting for transfers between devices, per_device(): mine = lax.all_to_all(part, 'dp', split_axis=0, concat_axis=0, tiled=True)  6.54 us
    unnamed x34, local copies, waits for them, and re-layouts  6.45 us
  transfers between devices with their start and end apart: 6, of which 5 were waited for; matrix products, arithmetic and copies ran while one was open for 1% of the time, Pallas kernels for 0%

commit v1 on v0

--- a/solution.py
+++ b/solution.py
@@ -6,6 +6,24 @@
 D = 2048
 HEAD_WIDTH = 128
 CAP = 6
+
+
+def ring_gather(array, axis, dim):
+    ways, here, step = (lax.axis_size(axis), lax.axis_index(axis), array.shape[dim])
+    lengths = [n * ways if d == dim else n for d, n in enumerate(array.shape)]
+    full = lax.dynamic_update_slice_in_dim(
+        jnp.zeros(lengths, array.dtype), array, here * step, axis=dim
+    )
+    going_up = going_down = array
+    for far in range(1, ways // 2 + 1):
+        going_up = lax.ppermute(going_up, axis, [(d, (d + 1) % ways) for d in range(ways)])
+        full = lax.dynamic_update_slice_in_dim(full, going_up, (here - far) % ways * step, axis=dim)
+        if 2 * far < ways:
+            going_down = lax.ppermute(going_down, axis, [(d, (d - 1) % ways) for d in range(ways)])
+            full = lax.dynamic_update_slice_in_dim(
+                full, going_down, (here + far) % ways * step, axis=dim
+            )
+    return full
 
 
 def attend_local(queries, fresh_keys, fresh_values, resident_keys, resident_values):
@@ -60,7 +78,7 @@
     half = D // lax.axis_size("tensor")
     groups = lax.axis_size("dp")
     attended = attend_local(queries, fresh_keys, fresh_values, resident_keys, resident_values)
-    gathered = lax.all_gather(attended, "dp", axis=0, tiled=True)
+    gathered = ring_gather(attended, "dp", 0)
     part = jnp.dot(gathered, out_weight, preferred_element_type=jnp.float32)
     part = part.reshape(groups, tokens_here, -1)
     mine = lax.all_to_all(part, "dp", split_axis=0, concat_axis=0, tiled=True)

time: 257 us -> 233 us (0.907)
  waiting for transfers between devices: 96.2 us -> 77.1 us
  between operations: 13.6 us -> 0.3 us
  starting transfers between devices: 14.8 us -> 19.2 us
    all_gather x1 -> x0, waiting for transfers between devices: 28.6 us -> none  [per_device(): gathered = lax.all_gather(attended, 'dp', axis=0, tiled=True)]
    ppermute x0 -> x3, waiting for transfers between devices: none -> 9.57 us  [the longest x2 9.56 us: ring_gather(): lax.ppermute(going_up, axis, [(d, (d + 1) % ways) for d in range(ways)])]
    ppermute x0 -> x3, starting transfers between devices: none -> 3.74 us  [the longest x2 2.99 us: ring_gather(): lax.ppermute(going_up, axis, [(d, (d + 1) % ways) for d in range(ways)])]
  transfers between devices with their start and end apart: 6 -> 8, of which waited for: 5 -> 6; matrix products, arithmetic and copies ran while one was open for 1% -> 2% of each run, Pallas kernels for 0% -> 0%
where the time goes in v1:
time: 233 us; the launch traced here: 232 us
  waiting for transfers between devices  77.1 us (33%)
  blocking collectives  67.3 us (29%)
  local copies, waits for them, and re-layouts  30.3 us (13%)
  matrix products  28.4 us (12%)
  starting transfers between devices  19.2 us (8%)
  other arithmetic  9.14 us (4%)
    all_to_all x1, blocking collectives, per_device(): lax.all_to_all(outgoing.reshape(owners, CAP, half), ('dp', 'expert'), spl...  67.3 us
    all_to_all x1, waiting for transfers between devices, per_device(): lax.all_to_all(expert_out.reshape(owners, CAP, half), ('dp', 'expert'), s...  51.7 us
    ppermute x2, waiting for transfers between devices, ring_gather(): lax.ppermute(going_up, axis, [(d, (d + 1) % ways) for d in range(ways)])  9.56 us
    dot_general x1, matrix products, per_device(): result = jnp.dot(act, w_down[0], preferred_element_type=jnp.float32)  9.28 us
    ppermute x3, waiting for transfers between devices, swap_pair(): return lax.ppermute(x, 'tensor', [(0, 1), (1, 0)])  9.27 us
    all_to_all x1, starting transfers between devices, per_device(): lax.all_to_all(expert_out.reshape(owners, CAP, half), ('dp', 'expert'), s...  9.03 us
    all_to_all x1, waiting for transfers between devices, per_device(): mine = lax.all_to_all(part, 'dp', split_axis=0, concat_axis=0, tiled=True)  6.54 us
    unnamed x34, local copies, waits for them, and re-layouts  6.44 us
  transfers between devices with their start and end apart: 8, of which 6 were waited for; matrix products, arithmetic and copies ran while one was open for 2% of the time, Pallas kernels for 0%

profile of v1, /device:TPU:2, one launch (start us, length us, event | category | flops | bytes accessed | tf_op | source)
XLA Modules:
  0.0 231.8 jit_solution(8581107260822255794)
XLA Ops:
  0.0 0.0 copy-start
  0.0 0.6 iota_add_fusion
  0.6 1.5 copy.47
  2.1 1.3 copy.48
  3.5 0.0 copy-done.5
  3.5 0.8 copy.62
  4.3 1.5 copy.44
  5.8 1.3 copy.45
  7.1 0.0 copy-done.8
  7.1 0.0 copy-done.9
  7.1 0.6 copy_bitcast_fusion.1
  7.8 0.8 fusion.27
  8.6 4.7 %fusion.48 = f32[2,8,64]{2,1,0:T(8,128)S(1)} fusion(pred[64,2112]{1,0:T(8,128)(4,1)S(1)} %fusion.27, bf16[64,2,128]{2,0,1:T(8,128)(2,1)} %get-tuple-element.9, bf16[2048,2,128]{2,0,1:T(8,128)(2,1)} %copy.48, bf16[64,2,8,128]{3,2,1,0:T(8,128)(2,1)S(1)} %bitcast.85), kind=kOutput, calls=%fused_computation.69 | convolution fusion | flops 564463680 | bytes 1482752 | tf_op jit(solution)/shard_map/sub | solution.py:49
  13.2 5.6 %fusion.14 = bf16[64,2,8,128]{3,0,2,1:T(8,128)(2,1)} fusion(f32[2,8,64]{2,1,0:T(8,128)S(1)} %fusion.48, bf16[64,2,128]{2,0,1:T(8,128)(2,1)} %get-tuple-element.10, bf16[2048,2,128]{2,0,1:T(8,128)(2,1)} %copy.45, pred[64,2112]{1,0:T(8,128)(4,1)S(1)} %fusion.27, bf16[64,2,128]{2,0,1:T(8,128)(2,1)} %get-tuple-element.9, ...), kind=kOutput, calls=%fused_computation.25 | convolution fusion | flops 1122569216 | bytes 2826240 | tf_op jit(solution)/shard_map/jgts,sjd->tjgd/dot_general | solution.py:51
  18.9 1.1 copy.51
  20.0 0.8 copy.80
  20.8 1.5 collective-permute-start
  22.3 0.8 collective-permute-start.1
  23.0 0.1 broadcast_in_dim.10
  23.1 0.1 constant_dynamic-update-slice_fusion.3
  23.2 5.9 %collective-permute-done = bf16[64,2048]{1,0:T(8,128)(2,1)} collective-permute-done((bf16[64,2048]{1,0:T(8,128)(2,1)}, bf16[64,2048]{1,0:T(8,128)(2,1)}, u32[]{:S(2)}, u32[]{:S(2)}) %collective-permute-start) | collective-permute-done | bytes 262176 | tf_op jit(solution)/shard_map/ppermute | solution.py:19
  29.1 1.5 collective-permute-start.2
  30.6 1.0 constant_dynamic-update-slice_fusion.2
  31.6 0.0 collective-permute-done.1
  31.6 1.0 constant_dynamic-update-slice_fusion.1
  32.6 3.7 %collective-permute-done.2 = bf16[64,2048]{1,0:T(8,128)(2,1)S(1)} collective-permute-done((bf16[64,2048]{1,0:T(8,128)(2,1)}, bf16[64,2048]{1,0:T(8,128)(2,1)S(1)}, u32[]{:S(2)}, u32[]{:S(2)}) %collective-permute-start.2) | collective-permute-done | bytes 262176 | tf_op jit(solution)/shard_map/ppermute | solution.py:19
  36.3 0.0 copy-start.10
  36.4 1.5 fusion.51
  37.8 6.0 %all-to-all-start = ((f32[4,64,512]{2,1,0:T(8,128)}), f32[4,64,512]{2,1,0:T(8,128)S(1)}, u32[]{:S(2)}, u32[]{:S(2)}) async-start(f32[4,64,512]{2,1,0:T(8,128)} %bitcast.83), calls=%async_computation | async-start | bytes 1048576 | tf_op jit(solution)/shard_map/all_to_all | solution.py:84
  43.8 0.1 copy.54
  43.9 6.5 %all-to-all-done = f32[4,64,512]{2,1,0:T(8,128)S(1)} async-done(((f32[4,64,512]{2,1,0:T(8,128)}), f32[4,64,512]{2,1,0:T(8,128)S(1)}, u32[]{:S(2)}, u32[]{:S(2)}) %all-to-all-start) | async-done | bytes 524320 | tf_op jit(solution)/shard_map/all_to_all | solution.py:84
  50.5 0.3 collective-permute-start.3
  50.8 0.1 convert_reduce_fusion
  50.9 0.1 reduce_window_sum.11
  51.0 1.2 select_reduce_fusion
  52.3 0.1 copy.55
  52.3 0.1 copy.56
  52.4 0.0 copy-done.12
  52.5 0.5 fusion.19
  53.0 0.0 collective-permute-done.3
  53.0 1.2 multiply_reduce_fusion.1
  54.3 1.8 convolution_convert_fusion
  56.0 3.7 %reshape.67 = bf16[128,6,1024]{2,1,0:T(8,128)(2,1)} reshape(bf16[768,1024]{1,0:T(8,128)(2,1)} %convolution_convert_fusion) | data formatting | bytes 3145728 | tf_op jit(solution)/shard_map/reshape | solution.py:104
  59.8 67.3 %all_to_all.15 = bf16[128,6,1024]{2,1,0:T(8,128)(2,1)} all-to-all(bf16[128,6,1024]{2,1,0:T(8,128)(2,1)} %reshape.67), channel_id=1, replica_groups=mesh['dp'=4,'expert'=32,'tensor'=2] {'dp','expert'}, dimensions={0} | all-to-all | bytes 3145728 | tf_op jit(solution)/shard_map/all_to_all | solution.py:103
  127.1 3.7 %reshape.68 = bf16[768,1024]{1,0:T(8,128)(2,1)} reshape(bf16[128,6,1024]{2,1,0:T(8,128)(2,1)} %all_to_all.15) | data formatting | bytes 3145728 | tf_op jit(solution)/shard_map/reshape | solution.py:109
  130.8 0.0 collective-permute-start.4
  130.8 3.7 %collective-permute-done.4 = bf16[768,1024]{1,0:T(8,128)(2,1)} collective-permute-done((bf16[768,1024]{1,0:T(8,128)(2,1)}, bf16[768,1024]{1,0:T(8,128)(2,1)}, u32[]{:S(2)}, u32[]{:S(2)}) %collective-permute-start.4) | collective-permute-done | bytes 1572896 | tf_op jit(solution)/shard_map/ppermute | solution.py:58
  134.5 2.1 broadcast_select_fusion.1
  136.7 1.2 copy-done.2
  137.9 0.4 copy-done.3
  138.3 2.8 %fusion.6 = f32[768,384]{1,0:T(8,128)} fusion(bf16[768,1024]{1,0:T(8,128)(2,1)S(1)} %get-tuple-element.8, bf16[768,1024]{1,0:T(8,128)(2,1)S(1)} %get-tuple-element.7, bf16[1,2048,384]{2,1,0:T(8,128)(2,1)S(1)} %copy-done.13), kind=kOutput, calls=%fused_computation.12 | convolution fusion | flops 1214251008 | bytes 5898240 | tf_op jit(solution)/shard_map/dot_general | solution.py:115
  141.1 9.3 %fusion.8 = f32[768,2048]{1,0:T(8,128)} fusion(bf16[1,384,2048]{2,1,0:T(8,128)(2,1)} %param.25, f32[768,384]{1,0:T(8,128)} %fusion.6, bf16[768,1024]{1,0:T(8,128)(2,1)} %copy-done.3, bf16[768,1024]{1,0:T(8,128)(2,1)} %copy-done.2, bf16[1,2048,384]{2,1,0:T(8,128)(2,1)} %param.23), kind=kOutput, calls=%fused_computation.15 | convolution fusion | flops 2423980032 | bytes 13762560 | tf_op jit(solution)/shard_map/dot_general | solution.py:117
  150.3 2.3 constant_dynamic-slice_fusion
  152.6 0.2 collective-permute-start.5
  152.8 5.5 %collective-permute-done.5 = f32[768,1024]{1,0:T(8,128)S(1)} collective-permute-done((f32[768,1024]{1,0:T(8,128)S(1)}, f32[768,1024]{1,0:T(8,128)S(1)}, u32[]{:S(2)}, u32[]{:S(2)}) %collective-permute-start.5) | collective-permute-done | bytes 3145760 | tf_op jit(solution)/shard_map/ppermute | solution.py:58
  158.4 1.7 add_convert_fusion
  160.0 3.7 %reshape.69 = bf16[128,6,1024]{2,1,0:T(8,128)(2,1)} reshape(bf16[768,1024]{1,0:T(8,128)(2,1)} %add_convert_fusion) | data formatting | bytes 3145728 | tf_op jit(solution)/shard_map/reshape | solution.py:122
  163.7 9.0 %all-to-all-start.2 = ((bf16[128,6,1024]{2,1,0:T(8,128)(2,1)}), bf16[128,6,1024]{2,1,0:T(8,128)(2,1)}, u32[]{:S(2)}, u32[]{:S(2)}) async-start(bf16[128,6,1024]{2,1,0:T(8,128)(2,1)} %reshape.69), calls=%async_computation.2 | async-start | bytes 4194304 | tf_op jit(solution)/shard_map/all_to_all | solution.py:121
  172.8 0.0 copy-done.11
  172.8 0.1 copy.53
  172.9 51.7 %all-to-all-done.2 = bf16[128,6,1024]{2,1,0:T(8,128)(2,1)} async-done(((bf16[128,6,1024]{2,1,0:T(8,128)(2,1)}), bf16[128,6,1024]{2,1,0:T(8,128)(2,1)}, u32[]{:S(2)}, u32[]{:S(2)}) %all-to-all-start.2) | async-done | bytes 1572896 | tf_op jit(solution)/shard_map/all_to_all | solution.py:121
  224.6 3.7 %reshape.73 = bf16[768,1024,1]{1,0,2:T(8,128)(2,1)} reshape(bf16[128,6,1024]{2,1,0:T(8,128)(2,1)} %all-to-all-done.2) | data formatting | bytes 3145728 | tf_op jit(solution)/shard_map/reshape | solution.py:127
  228.3 2.8 %multiply_reduce_fusion = f32[64,1024]{1,0:T(8,128)S(1)} fusion(bf16[768,1024,1]{1,0,2:T(8,128)(2,1)} %reshape.73, f32[64,8]{1,0:T(8,128)S(1)} %copy.53, s32[64,8]{1,0:T(8,128)S(1)} %copy.56), kind=kOutput, calls=%fused_computation.11 | convolution fusion | flops 806682624 | bytes 1839104 | tf_op jit(solution)/shard_map/tkr,rf->tkf/dot_general | solution.py:128
  231.1 0.7 add_convert_fusion.1
  (26 shorter events, 0.1 us)
Async XLA Ops:
  0.0 36.3 %copy-start = (bf16[2048,512]{1,0:T(8,128)(2,1)S(1)}, bf16[2048,512]{1,0:T(8,128)(2,1)}, u32[]{:S(2)}) copy-start(bf16[2048,512]{1,0:T(8,128)(2,1)} %param.18) | copy-start | bytes 6291460
  0.6 2.9 %copy-start.5 = (bf16[64,2048]{1,0:T(8,128)(2,1)S(1)}, bf16[64,2048]{1,0:T(8,128)(2,1)}, u32[]{:S(2)}) copy-start(bf16[64,2048]{1,0:T(8,128)(2,1)} %param.13) | copy-start | bytes 786436
  4.3 2.9 %copy-start.8 = (bf16[64,256]{1,0:T(8,128)(2,1)S(1)}, bf16[64,256]{1,0:T(8,128)(2,1)}, u32[]{:S(2)}) copy-start(bf16[64,256]{1,0:T(8,128)(2,1)} %param.15) | copy-start | bytes 98308
  4.3 2.9 %copy-start.9 = (bf16[64,256]{1,0:T(8,128)(2,1)S(1)}, bf16[64,256]{1,0:T(8,128)(2,1)}, u32[]{:S(2)}) copy-start(bf16[64,256]{1,0:T(8,128)(2,1)} %param.14) | copy-start | bytes 98308
  4.3 4.3 %copy-start.6 = (bf16[8,8,16,128]{3,2,1,0:T(8,128)(2,1)S(1)}, bf16[8,8,16,128]{3,2,1,0:T(8,128)(2,1)}, u32[]{:S(2)}) copy-start(bf16[8,8,16,128]{3,2,1,0:T(8,128)(2,1)} %copy.62) | copy-start | bytes 786436
  8.6 4.7 %copy-start.4 = (bf16[2048,2,128]{2,0,1:T(8,128)(2,1)S(1)}, bf16[2048,2,128]{2,0,1:T(8,128)(2,1)}, u32[]{:S(2)}) copy-start(bf16[2048,2,128]{2,0,1:T(8,128)(2,1)} %copy.48) | copy-start | bytes 3145732
  20.8 8.4 %collective-permute-start = (bf16[64,2048]{1,0:T(8,128)(2,1)}, bf16[64,2048]{1,0:T(8,128)(2,1)}, u32[]{:S(2)}, u32[]{:S(2)}) collective-permute-start(bf16[64,2048]{1,0:T(8,128)(2,1)} %bitcast.75), channel_id=1, source_target_pairs={{0,64},{64,128},{128,192},{192,0},{1,65},{65,129},{129,193},{193,1... | collective-permute-start | bytes 786440 | tf_op jit(solution)/shard_map/ppermute | solution.py:19
  22.3 9.4 %collective-permute-start.1 = (bf16[64,2048]{1,0:T(8,128)(2,1)}, bf16[64,2048]{1,0:T(8,128)(2,1)}, u32[]{:S(2)}, u32[]{:S(2)}) collective-permute-start(bf16[64,2048]{1,0:T(8,128)(2,1)} %bitcast.75), channel_id=1, source_target_pairs={{0,192},{64,0},{128,64},{192,128},{1,193},{65,1},{129,65},{193,129... | collective-permute-start | bytes 786440 | tf_op jit(solution)/shard_map/ppermute | solution.py:22
  29.1 7.2 %collective-permute-start.2 = (bf16[64,2048]{1,0:T(8,128)(2,1)}, bf16[64,2048]{1,0:T(8,128)(2,1)S(1)}, u32[]{:S(2)}, u32[]{:S(2)}) collective-permute-start(bf16[64,2048]{1,0:T(8,128)(2,1)} %collective-permute-done), channel_id=1, source_target_pairs={{0,64},{64,128},{128,192},{192,0},{1,65},{65,129},{129,193},{193,1... | collective-permute-start | bytes 786440 | tf_op jit(solution)/shard_map/ppermute | solution.py:19
  36.3 7.5 %copy-start.10 = (s32[64,8]{0,1:T(8,128)S(1)}, s32[64,8]{0,1:T(8,128)}, u32[]{:S(2)}) copy-start(s32[64,8]{0,1:T(8,128)} %param.21) | copy-start | bytes 6148
  37.8 14.6 %copy-start.12 = (f32[2048]{0:T(1024)S(1)}, f32[2048]{0:T(1024)}, u32[]{:S(2)}) copy-start(f32[2048]{0:T(1024)} %param.20) | copy-start | bytes 24580
  37.8 15.2 %copy-start.7 = (bf16[64,2048]{1,0:T(8,128)(2,1)S(1)}, bf16[64,2048]{1,0:T(8,128)(2,1)}, u32[]{:S(2)}) copy-start(bf16[64,2048]{1,0:T(8,128)(2,1)} %param.19) | copy-start | bytes 786436
  37.8 12.6 %all-to-all-start = ((f32[4,64,512]{2,1,0:T(8,128)}), f32[4,64,512]{2,1,0:T(8,128)S(1)}, u32[]{:S(2)}, u32[]{:S(2)}) async-start(f32[4,64,512]{2,1,0:T(8,128)} %bitcast.83), calls=%async_computation | async-start | bytes 1048576 | tf_op jit(solution)/shard_map/all_to_all | solution.py:84
  50.5 2.5 %collective-permute-start.3 = (f32[64,2048]{1,0:T(8,128)S(1)}, f32[64,2048]{1,0:T(8,128)}, u32[]{:S(2)}, u32[]{:S(2)}) collective-permute-start(f32[64,2048]{1,0:T(8,128)S(1)} %bitcast.81), channel_id=1, source_target_pairs={{0,1},{1,0},{2,3},{3,2},{4,5},{5,4},{6,7},{7,6},{8,9},{9,8},{10,11... | collective-permute-start | bytes 1572872 | tf_op jit(solution)/shard_map/ppermute | solution.py:58
  130.8 3.8 %collective-permute-start.4 = (bf16[768,1024]{1,0:T(8,128)(2,1)}, bf16[768,1024]{1,0:T(8,128)(2,1)}, u32[]{:S(2)}, u32[]{:S(2)}) collective-permute-start(bf16[768,1024]{1,0:T(8,128)(2,1)} %reshape.68), channel_id=1, source_target_pairs={{0,1},{1,0},{2,3},{3,2},{4,5},{5,4},{6,7},{7,6},{8,9},{9,8},{10,11... | collective-permute-start | bytes 4718600 | tf_op jit(solution)/shard_map/ppermute | solution.py:58
  130.8 7.5 %copy-start.13 = (bf16[1,2048,384]{2,1,0:T(8,128)(2,1)S(1)}, bf16[1,2048,384]{2,1,0:T(8,128)(2,1)}, u32[]{:S(2)}) copy-start(bf16[1,2048,384]{2,1,0:T(8,128)(2,1)} %param.24) | copy-start | bytes 4718596
  136.6 1.2 copy-start.2
  136.6 1.6 copy-start.3
  150.3 8.0 %copy-start.1 = (f32[768,2048]{1,0:T(8,128)S(1)}, f32[768,2048]{1,0:T(8,128)}, u32[]{:S(2)}) copy-start(f32[768,2048]{1,0:T(8,128)} %fusion.8) | copy-start | bytes 18874372
  152.6 5.7 %collective-permute-start.5 = (f32[768,1024]{1,0:T(8,128)S(1)}, f32[768,1024]{1,0:T(8,128)S(1)}, u32[]{:S(2)}, u32[]{:S(2)}) collective-permute-start(f32[768,1024]{1,0:T(8,128)S(1)} %constant_dynamic-slice_fusion), channel_id=1, source_target_pairs={{0,1},{1,0},{2,3},{3,2},{4,5},{5,4},{6,7},{7,6},{8,9},{9,8},{10,11... | collective-permute-start | bytes 9437192 | tf_op jit(solution)/shard_map/ppermute | solution.py:58
  163.7 9.0 %copy-start.11 = (f32[64,8]{0,1:T(8,128)S(1)}, f32[64,8]{0,1:T(8,128)}, u32[]{:S(2)}) copy-start(f32[64,8]{0,1:T(8,128)} %param.22) | copy-start | bytes 6148
  163.7 60.9 %all-to-all-start.2 = ((bf16[128,6,1024]{2,1,0:T(8,128)(2,1)}), bf16[128,6,1024]{2,1,0:T(8,128)(2,1)}, u32[]{:S(2)}, u32[]{:S(2)}) async-start(bf16[128,6,1024]{2,1,0:T(8,128)(2,1)} %reshape.69), calls=%async_computation.2 | async-start | bytes 4194304 | tf_op jit(solution)/shard_map/all_to_all | solution.py:121
